TPU v7x, 256 devices: a whole 4x4x8 slice. The times are simulated.
256 devices in a mesh: wide: 32 (over y, x, core), narrow: 8 (over z).
Axes of the slice: x: 4, y: 4, z: 8, core: 2. Of those that a mesh axis runs over, the one named last changes fastest.
Arguments:
- constraint_rows: bfloat16 [512, 256, 1024], P(None, ('wide', 'narrow')), may hold values from -1 to 1
- metric: bfloat16 [1024, 1024], replicated, may hold values from -8 to 8, as said below
Outputs:
- factored: float32 [512, 256, 8, 128], P(None, 'wide', 'narrow')
Inputs may be any that keep to these rules, and one draw needn't show every extreme that they name: `metric`: symmetric and positive definite.
All inputs are finite; a program needn't handle non-finite values.
Results may differ from a plain program's by a relative error of at most 0.0052.
Values may be sent and summed in bfloat16 or wider, within the bound.
No kernel may reach another device: no remote copies, remote signals or barrier semaphores. Data moves between devices by JAX's collectives and lax.ppermute only.
A program may use at most 64 MiB of HBM per device.

v0:
```python
import jax
import jax.numpy as jnp
from jax import lax
from jax.sharding import PartitionSpec as P

P_SIZE = 1024
PB = 256
NPANEL = 2


def left_solve(factor_low, right_side):
    return jax.scipy.linalg.solve_triangular(factor_low, right_side, lower=True)


def strip_major(schur_slab, strips):
    row_count = schur_slab.shape[0]
    strip_len = schur_slab.shape[1] // strips
    reordered = schur_slab.reshape(row_count, strip_len, strips).transpose(0, 2, 1)
    return reordered.reshape(row_count, 1, strips, strip_len)


def local(constraint_rows, metric):
    groups = lax.axis_size(("wide", "narrow"))
    strips = lax.axis_size("narrow")
    row_count = constraint_rows.shape[0]
    panel_depth = P_SIZE // groups
    block_rows = PB // groups
    flat_rows = constraint_rows[:, 0, :]
    projected = jnp.dot(flat_rows, metric, preferred_element_type=jnp.float32).astype(jnp.bfloat16)
    gram_cols = jnp.einsum(
        "rn,kmn->rkm",
        projected,
        lax.all_gather(constraint_rows[:panel_depth], ("wide", "narrow"), axis=1, tiled=True),
        preferred_element_type=jnp.float32,
    )
    schur_slab = (gram_cols * gram_cols).reshape(row_count, P_SIZE)
    grid_block = lax.all_to_all(
        strip_major(schur_slab, strips), "narrow", split_axis=2, concat_axis=1, tiled=True
    )
    strip_len = P_SIZE // strips
    grid_rows = row_count * strips
    narrow_panel = PB // strips
    own_strip = lax.axis_index("narrow")
    flat_block = grid_block.reshape(grid_rows, strip_len)
    for panel_number in range(NPANEL):
        col_begin = panel_number * PB
        row_begin = col_begin // groups
        strip_begin = col_begin // strips
        strip_end = strip_begin + narrow_panel
        own_rows = flat_block.reshape(row_count, strips, strip_len)[
            row_begin : row_begin + block_rows, :, strip_begin:
        ]
        shared = lax.all_gather(own_rows, "wide", axis=1, tiled=True)
        shared = shared.reshape(PB, strip_len - strip_begin)
        diag_strip, row_strip = (
            lax.all_gather(shared[:, :narrow_panel], "narrow", axis=1, tiled=True),
            lax.all_gather(flat_block[:, strip_begin:strip_end], "narrow", axis=1, tiled=True),
        )
        diag_block = diag_strip.reshape(PB, strips, narrow_panel).transpose(0, 2, 1).reshape(PB, PB)
        panel_cols = (
            row_strip.reshape(grid_rows, strips, narrow_panel)
            .transpose(0, 2, 1)
            .reshape(grid_rows, PB)
        )
        factor_low = jnp.linalg.cholesky(diag_block)
        upper_part = left_solve(factor_low, shared[:, narrow_panel:])
        column = left_solve(factor_low, panel_cols.T).T
        trailing = flat_block[:, strip_end:] - jnp.dot(
            column, upper_part, precision=lax.Precision.HIGHEST
        )
        own_cols = lax.dynamic_index_in_dim(
            column.reshape(grid_rows, narrow_panel, strips), own_strip, 2, keepdims=False
        )
        flat_block = jnp.concatenate([flat_block[:, :strip_begin], own_cols, trailing], axis=1)
    return flat_block.reshape(row_count, strips, 1, strip_len)


def solution(mesh):
    placed = (P(None, ("wide", "narrow"), None), P())
    return jax.shard_map(
        local,
        mesh=mesh,
        in_specs=placed,
        out_specs=P(None, "wide", "narrow", None),
        check_vma=False,
    )
```

profile of v0, /device:TPU:4, one launch (start us, length us, event | category | flops | bytes accessed | tf_op | source)
XLA Modules:
  0.0 463.7 jit_solution(18273028846116087548)
XLA Ops:
  6.5 1.5 slice.104
  8.1 110.0 %all-gather.6.cloned.1.call-done = bf16[4,256,1024]{2,0,1:T(4,128)(2,1)} async-done(((bf16[4,1,1024]{2,0,1:T(4,128)(2,1)}), bf16[4,256,1024]{2,0,1:T(4,128)(2,1)}) %all-gather.6.cloned.1.call-update) | async-done | bytes 2097168 | tf_op jit(solution)/shard_map/all_gather | solution.py:33
  118.1 5.7 %fusion.8 = f32[512,4,256]{0,2,1:T(8,128)} fusion(bf16[4,256,1024]{2,0,1:T(4,128)(2,1)} %all-gather.6.cloned.1.call-done, bf16[1024,1024]{1,0:T(8,128)(2,1)S(1)} %copy-done, bf16[512,1,1024]{2,0,1:T(8,128)(2,1)} %param.5), kind=kOutput, calls=%fused_computation.22 | convolution fusion | flops 2148532224 | bytes 7340032 | tf_op jit(solution)/shard_map/rn,kmn->rkm/dot_general | solution.py:30
  123.8 2.0 copy.62
  125.8 56.3 %all_to_all.4 = f32[512,1,8,128]{3,1,0,2:T(1,128)S(1)} all-to-all(f32[512,1,8,128]{3,1,0,2:T(1,128)S(1)} %bitcast.153), channel_id=1, replica_groups=mesh['wide'=32,'narrow'=8] {'narrow'}, dimensions={2} | all-to-all | bytes 4194304 | tf_op jit(solution)/shard_map/all_to_all | solution.py:37
  182.1 1.2 copy.100
  183.4 1.4 copy.68
  184.9 1.9 slice.153
  186.8 23.0 %all-gather = f32[1,1,256,128]{3,2,1,0:T(8,128)S(1)} all-gather(f32[1,1,8,128]{3,2,1,0:T(8,128)S(1)} %bitcast.150), channel_id=2, replica_groups=mesh['wide'=32,'narrow'=8] {'wide'}, dimensions={2}, use_global_device_ids=true | all-gather | bytes 135168 | tf_op jit(solution)/shard_map/all_gather | solution.py:53
  210.1 26.7 %all_gather.23 = f32[256,256]{0,1:T(8,128)S(1)} all-gather(f32[256,32]{0,1:T(8,128)S(1)} %copy.64), channel_id=1, replica_groups=mesh['wide'=32,'narrow'=8] {'narrow'}, dimensions={1}, use_global_device_ids=true | all-gather | bytes 294912 | tf_op jit(solution)/shard_map/all_gather | solution.py:56
  237.3 11.7 %cholesky.130 = f32[128,128]{1,0:T(8,128)S(1)} custom-call(f32[128,128]{1,0:T(8,128)S(1)} %cholesky.194), custom_call_target="Cholesky" | custom-call | tf_op jit(solution)/shard_map/jit(cholesky)/cholesky | solution.py:65
  249.1 9.8 %custom-call.23 = f32[1,128,128]{1,2,0:T(8,128)S(1)} custom-call(f32[1,128,128]{2,1,0:T(8,128)S(1)} %get-tuple-element.66), custom_call_target="InvertDiagBlocksLowerTriangular" | custom-call | tf_op jit(solution)/shard_map/jit(cholesky)/cholesky | solution.py:65
  258.9 0.2 constant_dynamic-update-slice_fusion.2
  259.1 0.3 convolution_subtract_fusion.5
  259.4 11.7 %cholesky.147 = f32[128,128]{1,0:T(8,128)S(1)} custom-call(f32[128,128]{1,0:T(8,128)S(1)} %convolution_subtract_fusion.5), custom_call_target="Cholesky" | custom-call | tf_op jit(solution)/shard_map/jit(cholesky)/cholesky | solution.py:65
  271.2 0.7 compare_reduce_fusion.2
  273.2 3.9 while.6
  273.2 0.6 fusion.60
  273.8 1.3 bitcast_dynamic-update-slice_fusion.4
  275.2 0.6 fusion.60
  275.8 1.3 bitcast_dynamic-update-slice_fusion.4
  277.1 19.7 %custom-call.24 = f32[2,128,128]{1,2,0:T(8,128)S(1)} custom-call(f32[2,128,128]{2,1,0:T(8,128)S(1)} %get-tuple-element.37), custom_call_target="InvertDiagBlocksLowerTriangular" | custom-call | tf_op jit(solution)/shard_map/jit(_solve_triangular)/triangular_solve | solution.py:12
  296.8 2.1 copy.83
  298.9 0.3 fusion.24
  299.3 0.3 convolution_subtract_fusion.6
  299.8 4.6 copy.99
  304.4 1.9 fusion.4
  306.3 2.0 convolution_subtract_fusion.1
  308.3 1.9 fusion.34
  310.3 2.7 convolution_subtract_fusion.2
  313.0 1.1 copy-done.5
  314.2 0.9 slice.156
  315.1 0.9 slice.154
  316.0 24.0 %all-gather.1 = f32[256,96]{1,0:T(8,128)S(1)} all-gather(f32[8,96]{1,0:T(8,128)S(1)} %copy.73), channel_id=3, replica_groups=mesh['wide'=32,'narrow'=8] {'wide'}, dimensions={0}, use_global_device_ids=true | all-gather | bytes 101376 | tf_op jit(solution)/shard_map/all_gather | solution.py:53
  340.2 26.5 %all_gather.26 = f32[256,256]{0,1:T(8,128)S(1)} all-gather(f32[256,32]{0,1:T(8,128)S(1)} %copy.85), channel_id=1, replica_groups=mesh['wide'=32,'narrow'=8] {'narrow'}, dimensions={1}, use_global_device_ids=true | all-gather | bytes 294912 | tf_op jit(solution)/shard_map/all_gather | solution.py:56
  367.2 11.7 %cholesky.164 = f32[128,128]{1,0:T(8,128)S(1)} custom-call(f32[128,128]{1,0:T(8,128)S(1)} %cholesky.197), custom_call_target="Cholesky" | custom-call | tf_op jit(solution)/shard_map/jit(cholesky)/cholesky | solution.py:65
  378.9 9.8 %custom-call.25 = f32[1,128,128]{1,2,0:T(8,128)S(1)} custom-call(f32[1,128,128]{2,1,0:T(8,128)S(1)} %get-tuple-element.62), custom_call_target="InvertDiagBlocksLowerTriangular" | custom-call | tf_op jit(solution)/shard_map/jit(cholesky)/cholesky | solution.py:65
  388.8 0.2 constant_dynamic-update-slice_fusion
  389.0 0.3 convolution_subtract_fusion.4
  389.3 11.7 %cholesky.181 = f32[128,128]{1,0:T(8,128)S(1)} custom-call(f32[128,128]{1,0:T(8,128)S(1)} %convolution_subtract_fusion.4), custom_call_target="Cholesky" | custom-call | tf_op jit(solution)/shard_map/jit(cholesky)/cholesky | solution.py:65
  401.0 0.6 compare_reduce_fusion.1
  401.7 0.7 compare_reduce_fusion
  403.6 3.9 while.7
  403.6 0.6 fusion.61
  404.2 1.3 bitcast_dynamic-update-slice_fusion.5
  405.6 0.6 fusion.61
  406.2 1.3 bitcast_dynamic-update-slice_fusion.5
  407.5 19.7 %custom-call.26 = f32[2,128,128]{1,2,0:T(8,128)S(1)} custom-call(f32[2,128,128]{2,1,0:T(8,128)S(1)} %get-tuple-element.38), custom_call_target="InvertDiagBlocksLowerTriangular" | custom-call | tf_op jit(solution)/shard_map/jit(_solve_triangular)/triangular_solve | solution.py:12
  427.2 2.0 fusion.1
  429.2 0.5 constant_dynamic-slice_fusion.3
  429.7 1.9 copy.70
  431.7 0.3 fusion.20
  432.0 0.2 convolution_subtract_fusion.7
  432.5 4.6 copy.98
  437.1 1.9 fusion.2
  439.0 2.0 convolution_subtract_fusion
  441.0 1.9 fusion.36
  443.0 0.4 fusion
  443.4 1.0 copy-done.6
  444.4 2.9 convolution_subtract_fusion.3
  447.2 0.5 constant_dynamic-slice_fusion.2
  447.7 2.0 copy.80
  449.7 1.7 copy.78
  451.5 5.5 %pad_maximum_fusion.4 = f32[512,8,1,128]{3,1,0,2:T(8,128)} fusion(f32[512,8,1,64]{3,1,0,2:T(8,128)} %bitcast.154, f32[512,8,1,32]{3,1,0,2:T(8,128)} %bitcast.152, f32[512,8,1,32]{3,1,0,2:T(8,128)} %bitcast.151), kind=kLoop, calls=%fused_computation.18 | loop fusion | flops 1048576 | bytes 4194304 | tf_op jit(solution)/shard_map/concatenate | solution.py:74
  (57 shorter events, 2.5 us)
Async XLA Ops:
  6.5 111.6 %copy-start = (bf16[1024,1024]{1,0:T(8,128)(2,1)S(1)}, bf16[1024,1024]{1,0:T(8,128)(2,1)}, u32[]{:S(2)}) copy-start(bf16[1024,1024]{1,0:T(8,128)(2,1)} %param.6) | copy-start | bytes 6291460
  6.5 111.6 %all-gather.6.cloned.1.call-start = ((), (), s32[]{:S(2)}) async-start(), calls=%async_computation.1 | async-start | bytes 2105344 | tf_op jit(solution)/shard_map/all_gather | solution.py:33
  8.0 291.7 %all-gather.8.cloned.1.call-start = ((), (), s32[]{:S(2)}) async-start(), calls=%async_computation.2 | async-start | bytes 4718592 | tf_op jit(solution)/shard_map/all_gather | solution.py:57
  182.1 1.3 copy-start.3
  184.8 247.6 %all-gather.10.cloned.1.call-start = ((), (), s32[]{:S(2)}) async-start(), calls=%async_computation.3 | async-start | bytes 4718592 | tf_op jit(solution)/shard_map/all_gather | solution.py:57
  184.9 1.9 slice-start
  237.0 59.8 %copy-start.4 = (f32[4096,96]{1,0:T(8,128)S(1)}, f32[4096,96]{1,0:T(8,128)}, u32[]{:S(2)}) copy-start(f32[4096,96]{1,0:T(8,128)} %slice.153) | copy-start | bytes 4718596
  308.3 2.0 copy-start.7
  310.3 2.8 copy-start.2
  313.0 1.1 copy-start.5
  442.9 1.4 copy-start.6
  451.5 5.5 %copy-start.1 = (bf16[1024,1024]{1,0:T(8,128)(2,1)S(1)}, bf16[1024,1024]{1,0:T(8,128)(2,1)}, u32[]{:S(2)}) copy-start(bf16[1024,1024]{1,0:T(8,128)(2,1)} %param.6) | copy-start | bytes 6291460
Sparse Core Ops, SparseCore 0:
  11.1 107.0 all-gather.5
  184.9 53.2 all-gather.7
  315.2 53.6 all-gather.9
where the time goes:
time: 469 us; the launch traced here: 464 us
  blocking collectives  157 us (33%)
  other arithmetic  116 us (25%)
  waiting for transfers between devices  110 us (23%)
  local copies, waits for them, and re-layouts  38.8 us (8%)
  matrix products  25.5 us (5%)
  between operations  16.2 us (3%)
    all_gather x1, waiting for transfers between devices, local(): lax.all_gather(constraint_rows[:panel_depth], ('wide', 'narrow'), axis=1,...  110 us
    another operation x13, other arithmetic, local(): factor_low = jnp.linalg.cholesky(diag_block)  68.6 us
    all_to_all x1, blocking collectives, local(): lax.all_to_all(strip_major(schur_slab, strips), 'narrow', split_axis=2, c...  56.3 us
    all_gather x2, blocking collectives, local(): lax.all_gather(shared[:, :narrow_panel], 'narrow', axis=1, tiled=True)  53.2 us
    all_gather x2, blocking collectives, local(): shared = lax.all_gather(own_rows, 'wide', axis=1, tiled=True)  47 us
    another operation x5, other arithmetic, left_solve(): return jax.scipy.linalg.solve_triangular(factor_low, right_side, lower=True)  39.4 us
    another operation x12, matrix products, left_solve(): return jax.scipy.linalg.solve_triangular(factor_low, right_side, lower=True)  13.2 us
  transfers between devices with their start and end apart: 3, of which 1 were waited for; matrix products, arithmetic and copies ran while one was open for 28% of the time, Pallas kernels for 0%

commit v1 on v0

--- a/solution.py
+++ b/solution.py
@@ -50,7 +50,8 @@
         own_rows = flat_block.reshape(row_count, strips, strip_len)[
             row_begin : row_begin + block_rows, :, strip_begin:
         ]
-        shared = lax.all_gather(own_rows, "wide", axis=1, tiled=True)
+        pieces = lax.all_gather(own_rows, "wide", axis=0, tiled=False)
+        shared = jnp.concatenate(pieces, axis=1)
         shared = shared.reshape(PB, strip_len - strip_begin)
         diag_strip, row_strip = (
             lax.all_gather(shared[:, :narrow_panel], "narrow", axis=1, tiled=True),

time: 469 us -> 471 us (level)
  no operation moved by 1% of the time
where the time goes in v1:
time: 471 us; the launch traced here: 465 us
  blocking collectives  157 us (33%)
  other arithmetic  116 us (25%)
  waiting for transfers between devices  110 us (23%)
  local copies, waits for them, and re-layouts  40.1 us (9%)
  matrix products  25.5 us (5%)
  between operations  16.4 us (3%)
    all_gather x1, waiting for transfers between devices, local(): lax.all_gather(constraint_rows[:panel_depth], ('wide', 'narrow'), axis=1,...  110 us
    another operation x13, other arithmetic, local(): factor_low = jnp.linalg.cholesky(diag_block)  68.7 us
    all_to_all x1, blocking collectives, local(): lax.all_to_all(strip_major(schur_slab, strips), 'narrow', split_axis=2, c...  56.3 us
    all_gather x2, blocking collectives, local(): lax.all_gather(shared[:, :narrow_panel], 'narrow', axis=1, tiled=True)  53.1 us
    all_gather x2, blocking collectives, local(): pieces = lax.all_gather(own_rows, 'wide', axis=0, tiled=False)  47.2 us
    another operation x5, other arithmetic, left_solve(): return jax.scipy.linalg.solve_triangular(factor_low, right_side, lower=True)  39.4 us
    another operation x12, matrix products, left_solve(): return jax.scipy.linalg.solve_triangular(factor_low, right_side, lower=True)  13.2 us
  transfers between devices with their start and end apart: 3, of which 1 were waited for; matrix products, arithmetic and copies ran while one was open for 28% of the time, Pallas kernels for 0%

profile of v1, /device:TPU:4, one launch (start us, length us, event | category | flops | bytes accessed | tf_op | source)
XLA Modules:
  0.0 465.2 jit_solution(17749053667751028280)
XLA Ops:
  6.5 1.5 slice.100
  8.1 110.0 %all-gather.5.cloned.1.call-done = bf16[4,256,1024]{2,0,1:T(4,128)(2,1)} async-done(((bf16[4,1,1024]{2,0,1:T(4,128)(2,1)}), bf16[4,256,1024]{2,0,1:T(4,128)(2,1)}) %all-gather.5.cloned.1.call-update) | async-done | bytes 2097168 | tf_op jit(solution)/shard_map/all_gather | solution.py:33
  118.1 5.7 %fusion.8 = f32[512,4,256]{0,2,1:T(8,128)} fusion(bf16[4,256,1024]{2,0,1:T(4,128)(2,1)} %all-gather.5.cloned.1.call-done, bf16[1024,1024]{1,0:T(8,128)(2,1)S(1)} %copy-done, bf16[512,1,1024]{2,0,1:T(8,128)(2,1)} %param.5), kind=kOutput, calls=%fused_computation.22 | convolution fusion | flops 2148532224 | bytes 7340032 | tf_op jit(solution)/shard_map/rn,kmn->rkm/dot_general | solution.py:30
  123.8 2.0 copy.62
  125.8 56.3 %all_to_all.4 = f32[512,1,8,128]{3,0,1,2:T(8,128)S(1)} all-to-all(f32[512,1,8,128]{3,0,1,2:T(8,128)S(1)} %bitcast.152), channel_id=1, replica_groups=mesh['wide'=32,'narrow'=8] {'narrow'}, dimensions={2} | all-to-all | bytes 4194304 | tf_op jit(solution)/shard_map/all_to_all | solution.py:37
  182.1 1.2 copy.99
  183.4 1.4 copy.68
  184.9 1.9 slice.147
  186.8 0.8 slice.144
  187.6 23.0 %all_gather.26 = f32[32,1,8,128]{3,2,1,0:T(8,128)S(1)} all-gather(f32[1,1,8,128]{3,2,1,0:T(8,128)S(1)} %bitcast.167), channel_id=1, replica_groups=mesh['wide'=32,'narrow'=8] {'wide'}, dimensions={0}, use_global_device_ids=true | all-gather | bytes 135168 | tf_op jit(solution)/shard_map/all_gather | solution.py:53
  210.9 26.6 %all_gather.27 = f32[256,256]{0,1:T(8,128)S(1)} all-gather(f32[256,32]{0,1:T(8,128)S(1)} %copy.64), channel_id=1, replica_groups=mesh['wide'=32,'narrow'=8] {'narrow'}, dimensions={1}, use_global_device_ids=true | all-gather | bytes 294912 | tf_op jit(solution)/shard_map/all_gather | solution.py:57
  238.0 11.7 %cholesky.130 = f32[128,128]{1,0:T(8,128)S(1)} custom-call(f32[128,128]{1,0:T(8,128)S(1)} %cholesky.194), custom_call_target="Cholesky" | custom-call | tf_op jit(solution)/shard_map/jit(cholesky)/cholesky | solution.py:66
  249.7 9.8 %custom-call.23 = f32[1,128,128]{1,2,0:T(8,128)S(1)} custom-call(f32[1,128,128]{2,1,0:T(8,128)S(1)} %get-tuple-element.66), custom_call_target="InvertDiagBlocksLowerTriangular" | custom-call | tf_op jit(solution)/shard_map/jit(cholesky)/cholesky | solution.py:66
  259.6 0.2 constant_dynamic-update-slice_fusion.2
  259.8 0.3 convolution_subtract_fusion.5
  260.1 11.7 %cholesky.147 = f32[128,128]{1,0:T(8,128)S(1)} custom-call(f32[128,128]{1,0:T(8,128)S(1)} %convolution_subtract_fusion.5), custom_call_target="Cholesky" | custom-call | tf_op jit(solution)/shard_map/jit(cholesky)/cholesky | solution.py:66
  271.8 0.7 compare_reduce_fusion.2
  274.0 4.2 while.6
  274.0 0.6 fusion.60
  274.6 1.4 bitcast_dynamic-update-slice_fusion.4
  276.1 0.6 fusion.60
  276.7 1.4 bitcast_dynamic-update-slice_fusion.4
  278.1 19.7 %custom-call.24 = f32[2,128,128]{1,2,0:T(8,128)S(1)} custom-call(f32[2,128,128]{2,1,0:T(8,128)S(1)} %get-tuple-element.37), custom_call_target="InvertDiagBlocksLowerTriangular" | custom-call | tf_op jit(solution)/shard_map/jit(_solve_triangular)/triangular_solve | solution.py:12
  297.8 2.1 copy.82
  299.9 0.3 fusion.24
  300.3 0.3 convolution_subtract_fusion.6
  300.8 4.6 copy.98
  305.4 1.9 fusion.4
  307.3 2.0 convolution_subtract_fusion.1
  309.3 1.9 fusion.34
  311.3 2.7 convolution_subtract_fusion.2
  314.0 1.1 copy-done.5
  315.2 0.9 slice.150
  316.1 0.9 slice.148
  317.0 24.1 %all-gather = f32[256,96]{1,0:T(8,128)S(1)} all-gather(f32[8,96]{1,0:T(8,128)S(1)} %copy.73), channel_id=2, replica_groups=mesh['wide'=32,'narrow'=8] {'wide'}, dimensions={0}, use_global_device_ids=true | all-gather | bytes 101376 | tf_op jit(solution)/shard_map/all_gather | solution.py:53
  341.3 26.5 %all_gather.31 = f32[256,256]{0,1:T(8,128)S(1)} all-gather(f32[256,32]{0,1:T(8,128)S(1)} %copy.84), channel_id=1, replica_groups=mesh['wide'=32,'narrow'=8] {'narrow'}, dimensions={1}, use_global_device_ids=true | all-gather | bytes 294912 | tf_op jit(solution)/shard_map/all_gather | solution.py:57
  368.3 11.7 %cholesky.164 = f32[128,128]{1,0:T(8,128)S(1)} custom-call(f32[128,128]{1,0:T(8,128)S(1)} %cholesky.197), custom_call_target="Cholesky" | custom-call | tf_op jit(solution)/shard_map/jit(cholesky)/cholesky | solution.py:66
  380.1 9.8 %custom-call.25 = f32[1,128,128]{1,2,0:T(8,128)S(1)} custom-call(f32[1,128,128]{2,1,0:T(8,128)S(1)} %get-tuple-element.62), custom_call_target="InvertDiagBlocksLowerTriangular" | custom-call | tf_op jit(solution)/shard_map/jit(cholesky)/cholesky | solution.py:66
  390.1 0.3 convolution_subtract_fusion.4
  390.4 11.7 %cholesky.181 = f32[128,128]{1,0:T(8,128)S(1)} custom-call(f32[128,128]{1,0:T(8,128)S(1)} %convolution_subtract_fusion.4), custom_call_target="Cholesky" | custom-call | tf_op jit(solution)/shard_map/jit(cholesky)/cholesky | solution.py:66
  402.1 0.7 compare_reduce_fusion.1
  402.8 0.7 compare_reduce_fusion
  404.9 4.1 while.7
  404.9 0.6 fusion.61
  405.5 1.4 bitcast_dynamic-update-slice_fusion.5
  406.9 0.6 fusion.61
  407.6 1.4 bitcast_dynamic-update-slice_fusion.5
  409.0 19.7 %custom-call.26 = f32[2,128,128]{1,2,0:T(8,128)S(1)} custom-call(f32[2,128,128]{2,1,0:T(8,128)S(1)} %get-tuple-element.38), custom_call_target="InvertDiagBlocksLowerTriangular" | custom-call | tf_op jit(solution)/shard_map/jit(_solve_triangular)/triangular_solve | solution.py:12
  428.7 2.0 fusion.1
  430.7 0.5 constant_dynamic-slice_fusion.3
  431.2 2.0 copy.70
  433.2 0.3 fusion.20
  433.5 0.2 convolution_subtract_fusion.7
  434.0 4.6 copy.97
  438.6 1.9 fusion.2
  440.5 2.0 convolution_subtract_fusion
  442.5 1.9 fusion.36
  444.5 0.4 fusion
  444.9 1.0 copy-done.6
  445.9 2.9 convolution_subtract_fusion.3
  448.8 0.5 constant_dynamic-slice_fusion.2
  449.3 1.9 copy.80
  451.2 1.7 copy.78
  452.9 5.5 %pad_maximum_fusion.4 = f32[512,8,1,128]{3,1,0,2:T(8,128)} fusion(f32[512,8,1,64]{3,1,0,2:T(8,128)} %bitcast.153, f32[512,8,1,32]{3,1,0,2:T(8,128)} %bitcast.151, f32[512,8,1,32]{3,1,0,2:T(8,128)} %bitcast.150), kind=kLoop, calls=%fused_computation.18 | loop fusion | flops 1048576 | bytes 4194304 | tf_op jit(solution)/shard_map/concatenate | solution.py:75
  (56 shorter events, 2.7 us)
Async XLA Ops:
  6.5 111.6 %copy-start = (bf16[1024,1024]{1,0:T(8,128)(2,1)S(1)}, bf16[1024,1024]{1,0:T(8,128)(2,1)}, u32[]{:S(2)}) copy-start(bf16[1024,1024]{1,0:T(8,128)(2,1)} %param.6) | copy-start | bytes 6291460
  6.5 111.6 %all-gather.5.cloned.1.call-start = ((), (), s32[]{:S(2)}) async-start(), calls=%async_computation.1 | async-start | bytes 2105344 | tf_op jit(solution)/shard_map/all_gather | solution.py:33
  8.0 292.7 %all-gather.7.cloned.1.call-start = ((), (), s32[]{:S(2)}) async-start(), calls=%async_computation.2 | async-start | bytes 4718592 | tf_op jit(solution)/shard_map/all_gather | solution.py:58
  182.1 1.3 copy-start.3
  184.8 249.1 %all-gather.9.cloned.1.call-start = ((), (), s32[]{:S(2)}) async-start(), calls=%async_computation.3 | async-start | bytes 4718592 | tf_op jit(solution)/shard_map/all_gather | solution.py:58
  237.6 60.2 %copy-start.4 = (f32[4096,96]{1,0:T(8,128)S(1)}, f32[4096,96]{1,0:T(8,128)}, u32[]{:S(2)}) copy-start(f32[4096,96]{1,0:T(8,128)} %slice.147) | copy-start | bytes 4718596
  309.3 2.0 copy-start.7
  311.3 2.8 copy-start.2
  314.0 1.1 copy-start.5
  444.5 1.4 copy-start.6
  452.9 5.5 %copy-start.1 = (bf16[1024,1024]{1,0:T(8,128)(2,1)S(1)}, bf16[1024,1024]{1,0:T(8,128)(2,1)}, u32[]{:S(2)}) copy-start(bf16[1024,1024]{1,0:T(8,128)(2,1)} %param.6) | copy-start | bytes 6291460
Sparse Core Ops, SparseCore 0:
  11.1 107.0 all-gather.4
  184.9 53.2 all-gather.6
  316.2 53.7 all-gather.8
